TPU v7x, 256 devices: a whole 4x4x8 slice. The times are simulated.
256 devices in a mesh: seq: 32 (over z, y), mp: 8 (over x, core).
Axes of the slice: x: 4, y: 4, z: 8, core: 2. Of those that a mesh axis runs over, the one named last changes fastest.
Arguments:
- tokens: bfloat16 [12288, 4096], P('seq', 'mp'), may hold values from -6 to 6
- norm_gain: float32 [2, 4096], replicated, may hold values from 0.25 to 1.75
- in_weight: bfloat16 [2, 3, 4096, 4096], P(None, None, 'seq', 'mp'), may hold values from -0.09375 to 0.09375
- feat_filter: float32 [2, 3, 3, 4096], P(None, None, None, 'mp'), may hold values from -3 to 3
- short_filter: float32 [256, 7], P('mp'), may hold values from -3 to 3
- medium_filter: float32 [256, 128], P('mp'), may hold values from -0.4 to 0.4
- out_weight: bfloat16 [4096, 4096], P('seq', 'mp'), may hold values from -0.09375 to 0.09375
Outputs:
- stream: bfloat16 [12288, 4096], P('seq', 'mp')
- mixed: bfloat16 [12288, 4096], P('seq', 'mp')
All inputs are finite; a program needn't handle non-finite values.
Results may differ from a plain program's by a relative error of at most 0.015.
Values may be sent and summed in bfloat16 or wider, within the bound.
A program may use at most 128 MiB of HBM per device.

v0:
```python
import jax
import jax.numpy as jnp
from jax import lax
from jax.sharding import PartitionSpec as P


def shifted(x, axis, by):
    peers = lax.axis_size(axis)
    pairs = [(i, i + by) for i in range(peers) if 0 <= i + by < peers]
    return lax.ppermute(x, axis, pairs)


def causal_taps(extended, taps, count):
    reach = taps.shape[0] - 1
    offset = extended.shape[0] - count - reach
    values = extended.astype(jnp.float32)
    total = jnp.zeros((count, extended.shape[1]), jnp.float32)
    for index in range(reach + 1):
        begin = offset + reach - index
        total = total + taps[index] * values[begin : begin + count]
    return total


def toeplitz_conv(kv_ext, filt, count):
    width = filt.shape[1]
    channels = kv_ext.shape[1]
    groups_here = filt.shape[0]
    per_group = channels // groups_here
    padded = jnp.concatenate([jnp.zeros((1, channels), kv_ext.dtype), kv_ext], axis=0)
    blocks = padded.astype(jnp.float32).reshape(count // width + 1, width, groups_here, per_group)
    lag = jnp.arange(width)[:, None] - jnp.arange(width)[None, :]
    current = jnp.where(lag >= 0, filt[:, jnp.clip(lag, 0, width - 1)], 0.0)
    earlier = jnp.where(lag < 0, filt[:, jnp.clip(lag + width, 0, width - 1)], 0.0)
    out = jnp.einsum("gik,bkgc->bigc", current, blocks[1:], precision=lax.Precision.HIGHEST)
    out = out + jnp.einsum("gik,bkgc->bigc", earlier, blocks[:-1], precision=lax.Precision.HIGHEST)
    return out.reshape(count, channels)


def normalized(stream_loc, gain):
    full = lax.all_gather(stream_loc, "mp", axis=1, tiled=True)
    values = full.astype(jnp.float32)
    mean_sq = jnp.mean(values * values, axis=-1, keepdims=True)
    return (values * lax.rsqrt(mean_sq + 1e-06) * gain).astype(jnp.bfloat16)


def project(normed, weights):
    return jnp.einsum(
        "rd,cdf->crf",
        normed,
        lax.all_gather(weights, "seq", axis=1, tiled=True),
        preferred_element_type=jnp.float32,
    ).astype(jnp.bfloat16)


def gated_mix(proj, feat_taps, inner_fn, span):
    rows = proj.shape[1]
    reach = feat_taps.shape[1] - 1
    rim = shifted(proj[:, rows - reach :, :], "seq", 1)
    extended = jnp.concatenate([rim, proj], axis=1)
    query = causal_taps(extended[0], feat_taps[0], rows)
    key_part = causal_taps(extended[1], feat_taps[1], rows)
    value_part = causal_taps(extended[2], feat_taps[2], rows)
    kv_prod = (key_part * value_part).astype(jnp.bfloat16)
    earlier = shifted(kv_prod[rows - span :], "seq", 1)
    kv_ext = jnp.concatenate([earlier, kv_prod], axis=0)
    inner = inner_fn(kv_ext, rows)
    return (query * inner).astype(jnp.bfloat16)


def local(tokens, norm_gain, in_weight, feat_filter, short_filter, medium_filter, out_weight):
    per_group = tokens.shape[1] // short_filter.shape[0]
    short_taps = jnp.repeat(short_filter.T, per_group, axis=1)

    def short_inner(kv_ext, count):
        return causal_taps(kv_ext, short_taps, count)

    def medium_inner(kv_ext, count):
        return toeplitz_conv(kv_ext, medium_filter, count)

    normed = normalized(tokens, norm_gain[0])
    proj = project(normed, in_weight[0])
    first = gated_mix(proj, feat_filter[0], short_inner, short_filter.shape[1] - 1)
    first_full = lax.all_gather(first, "mp", axis=1, tiled=True)
    delta = jnp.dot(
        first_full,
        lax.all_gather(out_weight, "seq", axis=0, tiled=True),
        preferred_element_type=jnp.float32,
    )
    stream = (tokens.astype(jnp.float32) + delta).astype(jnp.bfloat16)
    normed_next = normalized(stream, norm_gain[1])
    proj_next = project(normed_next, in_weight[1])
    mixed = gated_mix(proj_next, feat_filter[1], medium_inner, medium_filter.shape[1] - 1)
    return (stream, mixed)


def solution(mesh):
    placed = (
        P("seq", "mp"),
        P(),
        P(None, None, "seq", "mp"),
        P(None, None, None, "mp"),
        P("mp", None),
        P("mp", None),
        P("seq", "mp"),
    )
    return jax.shard_map(
        local,
        mesh=mesh,
        in_specs=placed,
        out_specs=(P("seq", "mp"), P("seq", "mp")),
        check_vma=False,
    )
```

profile of v0, /device:TPU:1, one launch (start us, length us, event | category | flops | bytes accessed | tf_op | source)
XLA Modules:
  0.0 595.5 jit_solution(11730328731184018714)
XLA Ops:
  7.9 2.1 fusion.119
  11.7 32.7 %all-gather.9.cloned.1.call-done = bf16[384,4096]{1,0:T(8,128)(2,1)} async-done(((bf16[384,512]{1,0:T(8,128)(2,1)}), bf16[384,4096]{1,0:T(8,128)(2,1)}) %all-gather.9.cloned.1.call-update) | async-done | bytes 3145744 | tf_op jit(solution)/shard_map/all_gather | solution.py:40
  44.4 2.7 fusion.4
  47.1 119.4 %all-gather.17.cloned.1.call-done = bf16[1,3,4096,512]{3,2,1,0:T(8,128)(2,1)} async-done(((bf16[1,3,128,512]{3,2,1,0:T(8,128)(2,1)}), bf16[1,3,4096,512]{3,2,1,0:T(8,128)(2,1)}) %all-gather.17.cloned.1.call-update) | async-done | bytes 12582928 | tf_op jit(solution)/shard_map/all_gather | solution.py:50
  166.5 8.2 %fusion.39 = bf16[3,384,512]{2,1,0:T(8,128)(2,1)S(1)} fusion(bf16[1,3,4096,512]{3,2,1,0:T(8,128)(2,1)} %all-gather.17.cloned.1.call-done, bf16[384,4096]{1,0:T(8,128)(2,1)S(1)} %copy-done.1, f32[4096]{0:T(1024)S(1)} %bitcast.255, f32[384]{0:T(512)S(1)} %add_rsqrt_fusion.1), kind=kOutput, calls=%fused_computation.35 | convolution fusion | flops 4838719488 | bytes 16926208 | tf_op jit(solution)/shard_map/rd,cdf->crf/dot_general | solution.py:47
  174.8 1.8 collective-permute-start
  178.2 3.6 collective-permute-start.1
  184.8 61.0 %all-gather.13.cloned.1.call-done = bf16[4096,512]{1,0:T(8,128)(2,1)} async-done(((bf16[128,512]{1,0:T(8,128)(2,1)}), bf16[4096,512]{1,0:T(8,128)(2,1)}) %all-gather.13.cloned.1.call-update) | async-done | bytes 4194320 | tf_op jit(solution)/shard_map/all_gather | solution.py:86
  245.8 32.9 %all-gather.11.cloned.1.call-done = bf16[384,4096]{1,0:T(8,128)(2,1)} async-done(((bf16[384,512]{1,0:T(8,128)(2,1)}), bf16[384,4096]{1,0:T(8,128)(2,1)}) %all-gather.11.cloned.1.call-update) | async-done | bytes 3145744 | tf_op jit(solution)/shard_map/all_gather | solution.py:83
  278.7 5.7 fusion.50
  285.0 29.9 %all-gather.15.cloned.1.call-done = bf16[384,4096]{1,0:T(8,128)(2,1)} async-done(((bf16[384,512]{1,0:T(8,128)(2,1)}), bf16[384,4096]{1,0:T(8,128)(2,1)}) %all-gather.15.cloned.1.call-update) | async-done | bytes 3145744 | tf_op jit(solution)/shard_map/all_gather | solution.py:40
  314.9 2.7 fusion.7
  317.7 119.3 %all-gather.19.cloned.1.call-done = bf16[1,3,4096,512]{3,2,1,0:T(8,128)(2,1)} async-done(((bf16[1,3,128,512]{3,2,1,0:T(8,128)(2,1)}), bf16[1,3,4096,512]{3,2,1,0:T(8,128)(2,1)}) %all-gather.19.cloned.1.call-update) | async-done | bytes 12582928 | tf_op jit(solution)/shard_map/all_gather | solution.py:50
  436.9 8.2 %fusion.34 = bf16[3,384,512]{2,1,0:T(8,128)(2,1)S(1)} fusion(bf16[1,3,4096,512]{3,2,1,0:T(8,128)(2,1)} %all-gather.19.cloned.1.call-done, bf16[384,4096]{1,0:T(8,128)(2,1)S(1)} %copy-done.2, f32[4096]{0:T(1024)S(1)} %bitcast.254, f32[384]{0:T(512)S(1)} %add_rsqrt_fusion), kind=kOutput, calls=%fused_computation.34 | convolution fusion | flops 4838719488 | bytes 16926208 | tf_op jit(solution)/shard_map/rd,cdf->crf/dot_general | solution.py:47
  445.2 1.8 collective-permute-start.2
  448.6 4.3 collective-permute-start.3
  453.6 54.8 %gather_fusion.1 = f32[16384,32]{1,0:T(8,128)} fusion(f32[32,128]{0,1:T(8,128)S(1)} %copy.17, s32[16384]{0:T(1024)S(1)} %fusion.114), kind=kCustom, calls=%fused_computation.1 | custom fusion | bytes 4259840 | tf_op jit(solution)/shard_map/gather | solution.py:33
  508.4 5.5 copy.22
  513.9 54.8 %gather_fusion = f32[16384,32]{1,0:T(8,128)} fusion(f32[32,128]{0,1:T(8,128)S(1)} %copy.17, s32[16384]{0:T(1024)S(1)} %fusion.112), kind=kCustom, calls=%fused_computation | custom fusion | bytes 4259840 | tf_op jit(solution)/shard_map/gather | solution.py:32
  568.7 6.4 %copy.18 = f32[128,128,32]{1,0,2:T(8,128)} copy(f32[128,128,32]{2,1,0:T(8,128)} %bitcast.250) | data formatting | bytes 4194304 | tf_op jit(solution)/shard_map/gather | solution.py:32
  576.1 2.0 slice.428
  578.1 1.8 pad_maximum_fusion.2
  582.0 2.9 fusion.18
  585.0 1.8 fusion.47
  (82 shorter events, 14.7 us)
Async XLA Ops:
  7.2 37.2 %all-gather.9.cloned.1.call-start = ((), (), s32[]{:S(2)}) async-start(), calls=%async_computation | async-start | bytes 3538944 | tf_op jit(solution)/shard_map/all_gather | solution.py:40
  7.9 158.6 %all-gather.17.cloned.1.call-start = ((), (), s32[]{:S(2)}) async-start(), calls=%async_computation.4 | async-start | bytes 12976128 | tf_op jit(solution)/shard_map/all_gather | solution.py:50
  10.0 235.8 %all-gather.13.cloned.1.call-start = ((), (), s32[]{:S(2)}) async-start(), calls=%async_computation.2 | async-start | bytes 4325376 | tf_op jit(solution)/shard_map/all_gather | solution.py:86
  10.8 267.9 %all-gather.11.cloned.1.call-start = ((), (), s32[]{:S(2)}) async-start(), calls=%async_computation.1 | async-start | bytes 3538944 | tf_op jit(solution)/shard_map/all_gather | solution.py:83
  44.4 122.2 %copy-start.1 = (bf16[384,4096]{1,0:T(8,128)(2,1)S(1)}, bf16[384,4096]{1,0:T(8,128)(2,1)}, u32[]{:S(2)}) copy-start(bf16[384,4096]{1,0:T(8,128)(2,1)} %all-gather.9.cloned.1.call-done) | copy-start | bytes 9437188
  166.5 10.1 %copy-start.6 = (f32[2,3,3,512]{3,0,2,1:T(2,128)S(1)}, f32[2,3,3,512]{3,0,2,1:T(2,128)}, u32[]{:S(2)}) copy-start(f32[2,3,3,512]{3,0,2,1:T(2,128)} %param.10) | copy-start | bytes 110596
  174.8 2.6 collective-permute-start
  177.6 4.2 copy-start.11
  178.2 4.7 collective-permute-start.1
  183.0 95.7 %copy-start.4 = (bf16[384,512]{1,0:T(8,128)(2,1)S(1)}, bf16[384,512]{1,0:T(8,128)(2,1)}, u32[]{:S(2)}) copy-start(bf16[384,512]{1,0:T(8,128)(2,1)} %param.7) | copy-start | bytes 1179652
  184.7 130.2 %all-gather.15.cloned.1.call-start = ((), (), s32[]{:S(2)}) async-start(), calls=%async_computation.3 | async-start | bytes 3538944 | tf_op jit(solution)/shard_map/all_gather | solution.py:40
  284.4 152.5 %all-gather.19.cloned.1.call-start = ((), (), s32[]{:S(2)}) async-start(), calls=%async_computation.5 | async-start | bytes 12976128 | tf_op jit(solution)/shard_map/all_gather | solution.py:50
  314.9 122.0 %copy-start.2 = (bf16[384,4096]{1,0:T(8,128)(2,1)S(1)}, bf16[384,4096]{1,0:T(8,128)(2,1)}, u32[]{:S(2)}) copy-start(bf16[384,4096]{1,0:T(8,128)(2,1)} %all-gather.15.cloned.1.call-done) | copy-start | bytes 9437188
  445.2 2.6 collective-permute-start.2
  448.0 5.5 copy-start.7
  448.6 129.5 %collective-permute-start.3 = (bf16[127,512]{1,0:T(8,128)(2,1)S(1)}, bf16[127,512]{1,0:T(8,128)(2,1)}, u32[]{:S(2)}, u32[]{:S(2)}) collective-permute-start(bf16[127,512]{1,0:T(8,128)(2,1)S(1)} %slice.472), channel_id=1, source_target_pairs={{0,8},{8,16},{16,24},{24,32},{32,40},{40,48},{48,56},{56,64},{64,7... | collective-permute-start | bytes 390152 | tf_op jit(solution)/shard_map/ppermute | solution.py:10
  575.1 6.9 %copy-start.5 = (pred[128,128]{1,0:T(8,128)(4,1)S(1)}, pred[128,128]{1,0:T(8,128)(4,1)}, u32[]{:S(2)}) copy-start(pred[128,128]{1,0:T(8,128)(4,1)} %fusion.115) | copy-start | bytes 49156
  582.0 3.0 copy-start
  582.0 3.0 copy-start.3
  586.8 0.8 copy-start.8
  586.8 0.8 copy-start.9
  586.8 0.8 copy-start.10
Sparse Core Ops, SparseCore 0:
  9.8 34.4 all-gather.8
  47.5 118.9 all-gather.16
  169.1 76.6 all-gather.12
  248.1 30.5 all-gather.10
  284.5 30.3 all-gather.14
  317.9 118.9 all-gather.18
where the time goes:
time: 598 us; the launch traced here: 595 us
  waiting for transfers between devices  398 us (67%)
  local copies, waits for them, and re-layouts  132 us (22%)
  matrix products  26.9 us (4%)
  between operations  14.4 us (2%)
  other arithmetic  12.3 us (2%)
  starting transfers between devices  11.7 us (2%)
    all_gather x2, waiting for transfers between devices, project(): lax.all_gather(weights, 'seq', axis=1, tiled=True)  239 us
    all_gather x2, waiting for transfers between devices, normalized(): full = lax.all_gather(stream_loc, 'mp', axis=1, tiled=True)  62.6 us
    gather x2, local copies, waits for them, and re-layouts, toeplitz_conv(): current = jnp.where(lag >= 0, filt[:, jnp.clip(lag, 0, width - 1)], 0.0)  61.2 us
    all_gather x1, waiting for transfers between devices, local(): lax.all_gather(out_weight, 'seq', axis=0, tiled=True)  61 us
    gather x2, local copies, waits for them, and re-layouts, toeplitz_conv(): filt[:, jnp.clip(lag + width, 0, width - 1)]  60.3 us
    all_gather x1, waiting for transfers between devices, local(): first_full = lax.all_gather(first, 'mp', axis=1, tiled=True)  32.9 us
    dot_general x2, matrix products, project(): jnp.einsum('rd,cdf->crf', normed, lax.all_gather(weights, 'seq', axis=1,...  16.5 us
  transfers between devices with their start and end apart: 10, of which 8 were waited for; matrix products, arithmetic and copies ran while one was open for 25% of the time, Pallas kernels for 0%

commit v1 on v0

v1 whole, which is shorter than its diff:
```python
import jax
import jax.numpy as jnp
from jax import lax
from jax.experimental import pallas as pl
from jax.experimental.pallas import tpu as pltpu
from jax.sharding import PartitionSpec as P

NY = 4
NX = 4
NZ = 8
LANES = 128
SPAN = 128


def remote(src, dst, send_sem, recv_sem, device):
    return pltpu.make_async_remote_copy(
        src_ref=src,
        dst_ref=dst,
        send_sem=send_sem,
        recv_sem=recv_sem,
        device_id=device,
        device_id_type=pl.DeviceIdType.MESH,
    )


class Gather:
    def __init__(self, buf, sems, index, at):
        self.buf, self.sems, self.index, self.at = buf, sems, index, at
        self.sent = []
        self.passed = []
        self.ids = {}

    def slot(self, dx, dy):
        at = self.at
        return (((at["x"] + dx + NX) % NX) * 2 + at["core"]) * NY + (at["y"] + dy + NY) % NY

    def number(self, key):
        return self.ids.setdefault(key, len(self.ids))

    def message(self, kind, part, step, off, rows):
        axis, sign = step
        physical = axis if part == 0 else 1 - axis
        offs = off if part == 0 else (off[1], off[0])
        half = self.buf.shape[1] // 4
        start, size = {"all": (0, 2), "lo": (0, 1), "hi": (1, 1)}[rows]
        span = pl.ds((2 * part + start) * half, size * half)
        key = self.number((part, step, off, rows))
        back = (offs[0] - sign, offs[1]) if physical == 0 else (offs[0], offs[1] - sign)
        where = self.at[("xp", "xm", "yp", "ym")[2 * physical + (0 if sign > 0 else 1)]]
        send, recv, csend, crecv = (self.sems.at[self.index, k, key] for k in range(4))
        here = self.buf.at[self.slot(*offs), span]
        there = self.buf.at[self.slot(*back), span]
        at = self.at
        other = (((at["x"] + back[0] + NX) % NX) * 2 + 1 - at["core"]) * NY + (at["y"] + back[1] + NY) % NY
        twin = self.buf.at[other, span]
        if kind == "send":
            return remote(here, here, send, recv, where)
        arrive = remote(there, there, send, recv, where)
        hand = remote(there, there, csend, crecv, at["cp"])
        handed = remote(twin, twin, csend, crecv, at["cp"])
        return arrive, hand, handed

    def send(self, *args):
        out = self.message("send", *args)
        out.start()
        self.sent.append(out)

    def receive(self, *args):
        arrive, hand, handed = self.message("receive", *args)
        arrive.wait_recv()
        hand.start()
        self.passed.append((hand, handed))

    def own(self):
        key = self.number("own")
        at = self.at
        here = self.buf.at[self.slot(0, 0)]
        twin = self.buf.at[(at["x"] * 2 + 1 - at["core"]) * NY + at["y"]]
        sems = self.sems.at[self.index, 2, key], self.sems.at[self.index, 3, key]
        hand = remote(here, here, *sems, at["cp"])
        hand.start()
        self.passed.append((hand, remote(twin, twin, *sems, at["cp"])))

    def steps(self):
        both = ((0, 1), (0, -1)), ((1, 1), (1, -1))

        def begin():
            for part in (0, 1):
                for step in both[0]:
                    self.send(part, step, (0, 0), "all")
            for part in (0, 1):
                for step in both[1]:
                    self.send(part, step, (0, 0), "all")
            self.own()

        def first():
            for sign in (1, -1):
                for part in (0, 1):
                    self.receive(part, (0, sign), (0, 0), "all")
                    self.send(part, (0, sign), (-sign, 0), "lo" if sign > 0 else "hi")
                    for step in both[1]:
                        self.send(part, step, (-sign, 0), "all")

        def across(a):
            def run():
                for part in (0, 1):
                    for sign in (1, -1):
                        self.receive(part, (1, sign), (a, 0), "all")
                        self.send(part, (1, sign), (a, -sign), "lo" if sign > 0 else "hi")
            return run

        def far():
            for part in (0, 1):
                for sign in (1, -1):
                    self.receive(part, (0, sign), (-sign, 0), "lo" if sign > 0 else "hi")
                for step in both[1]:
                    self.send(part, step, (2, 0), "all")

        def last(a):
            def run():
                for part in (0, 1):
                    for sign in (1, -1):
                        self.receive(part, (1, sign), (a, -sign), "lo" if sign > 0 else "hi")
            return run

        def end():
            for hand, handed in self.passed:
                handed.wait_recv()

        return [begin, first, across(0), far, across(-1), across(1), last(0), across(2), last(-1), last(1), last(2), end]

    def drain(self):
        for out in self.sent:
            out.wait_send()
        for hand, _ in self.passed:
            hand.wait_send()


class Ring:
    def __init__(self, buf, stage, first, sems, index, at, local_sem):
        self.buf, self.sems, self.index, self.at = buf, sems, index, at
        self.stage, self.first, self.local_sem = stage, first, local_sem
        self.sent = []
        self.count = buf.shape[1]

    def trade(self):
        at = self.at
        rows = pl.ds(at["y"] * LANES, LANES)
        dst = self.buf.at[at["z"], :, rows]
        part = pl.ds(self.first, self.count)
        self.mine = pltpu.make_async_copy(
            self.stage.at[part, :, pl.ds(pl.multiple_of(at["y"] * LANES, LANES), LANES)], dst, self.local_sem
        )
        self.mine.start()
        for d in (1, 3, 2):
            to = (at["y"] + d) % NY
            src = self.stage.at[part, :, pl.ds(pl.multiple_of(to * LANES, LANES), LANES)]
            out = remote(src, dst, self.sems.at[self.index, 0, d], self.sems.at[self.index, 1, d], at["y%d" % d])
            out.start()
            self.sent.append(out)

    def block(self, z_off, part):
        at = self.at
        ref = self.buf.at[(at["z"] + z_off + NZ) % NZ]
        if part == "all":
            return ref
        half = ref.shape[1] // 2
        return ref.at[:, pl.ds(0 if part == "lo" else half, half)]

    def copy(self, sign, s, received):
        part = "all" if s < 3 else ("lo" if sign > 0 else "hi")
        ref = self.block(-sign * (s + (1 if received else 0)), part)
        k = 4 + (0 if sign > 0 else 4) + s
        return remote(ref, ref, self.sems.at[self.index, 0, k], self.sems.at[self.index, 1, k], self.at["zp" if sign > 0 else "zm"])

    def send(self, sign, s):
        out = self.copy(sign, s, False)
        out.start()
        self.sent.append(out)

    def steps(self):
        def begin():
            at = self.at
            self.mine.wait()
            for d in (1, 3, 2):
                rows = pl.ds(((at["y"] + NY - d) % NY) * LANES, LANES)
                ref = self.buf.at[at["z"], :, rows]
                remote(ref, ref, self.sems.at[self.index, 0, d], self.sems.at[self.index, 1, d], at["y%d" % d]).wait_recv()
            self.send(1, 0)
            self.send(-1, 0)

        def step(s):
            def run():
                for sign in (1, -1):
                    self.copy(sign, s - 1, True).wait_recv()
                    if s < 4:
                        self.send(sign, s)
            return run

        return [begin] + [step(s) for s in (1, 2, 3, 4)]

    def drain(self):
        for out in self.sent:
            out.wait_send()


def kernel(tok, gain, w_in, taps, filt, w_out, stream_ref, mixed_ref,
           xbuf, ybuf, sbuf, w0, wo, w1, stage, gcol, tap, fil, toep, proj, rim, tail, kv, mix,
           gsem, wsem, hsem, osem, lsem):
    seq = lax.axis_index("seq")
    mp = lax.axis_index("mp")
    y, z = seq % NY, seq // NY
    x, core = mp // 2, mp % 2
    at = {"x": x, "y": y, "z": z, "core": core}
    at["xp"] = {"mp": ((x + 1) % NX) * 2 + core}
    at["xm"] = {"mp": ((x + NX - 1) % NX) * 2 + core}
    at["cp"] = {"mp": x * 2 + 1 - core}
    for d in (1, 2, 3):
        at["y%d" % d] = {"seq": z * NY + (y + d) % NY}
    at["yp"], at["ym"] = at["y1"], at["y3"]
    at["zp"] = {"seq": ((z + 1) % NZ) * NY + y}
    at["zm"] = {"seq": ((z + NZ - 1) % NZ) * NY + y}
    own = mp * NY + y
    rows = tok.shape[0]
    total = rows * NY

    loads = [
        pltpu.make_async_copy(tok.at[:, pl.ds(LANES * i, LANES)], xbuf.at[own, pl.ds(rows * i, rows)], lsem.at[i])
        for i in range(4)
    ]
    loads.append(pltpu.make_async_copy(w_in.at[0], stage.at[pl.ds(0, 3)], lsem.at[4]))
    loads.append(pltpu.make_async_copy(w_out, stage.at[3], lsem.at[5]))
    loads.append(pltpu.make_async_copy(w_in.at[1], stage.at[pl.ds(4, 3)], lsem.at[6]))
    loads.append(pltpu.make_async_copy(gain.at[:, pl.ds(pl.multiple_of(seq * LANES, LANES), LANES)], gcol, lsem.at[7]))
    loads.append(pltpu.make_async_copy(taps.at[:, pl.ds(pl.multiple_of(y * LANES, LANES), LANES)], tap, lsem.at[8]))
    loads.append(pltpu.make_async_copy(filt.at[:, pl.ds(pl.multiple_of(y * 8, 8), 8)], fil, lsem.at[9]))
    for c in loads:
        c.start()

    barrier = pltpu.get_barrier_semaphore()
    peers = ("xp", "xm", "cp", "y1", "y2", "y3", "zp", "zm")
    for name in peers:
        pl.semaphore_signal(barrier, inc=1, device_id=at[name], device_id_type=pl.DeviceIdType.MESH)
    for c in loads:
        c.wait()
    pl.semaphore_wait(barrier, len(peers))

    gathers = [Gather(buf, gsem, i, at) for i, buf in enumerate((xbuf, ybuf, sbuf))]
    gx, gy, gs = gathers
    rings = [
        Ring(w0, stage, 0, wsem, 0, at, lsem.at[0]),
        Ring(wo, stage, 3, wsem, 1, at, lsem.at[1]),
        Ring(w1, stage, 4, wsem, 2, at, lsem.at[2]),
    ]
    rs = [r.steps() for r in rings]

    def scale(block):
        column = jnp.transpose(jnp.broadcast_to(gcol[block : block + 1, :], (LANES, LANES)))
        for c in range(3):
            for j in range(4):
                lanes = pl.ds(LANES * j, LANES)
                value = stage[4 * block + c, :, lanes].astype(jnp.float32) * column
                stage[4 * block + c, :, lanes] = value.astype(jnp.bfloat16)

    def build(block):
        for g in range(8):
            line = jnp.broadcast_to(fil[block, g : g + 1, :], (2 * SPAN, 2 * SPAN))
            skew = pltpu.roll(line, SPAN, 1, stride=1, stride_axis=0)
            toep[block, pl.ds(SPAN * g, SPAN), :] = jnp.transpose(skew[:, :SPAN]).astype(jnp.bfloat16)

    def operand(buf, tile, tokens_form):
        if tokens_form:
            pieces = [buf[m * NY + tile, pl.ds(rows * j, rows), :] for m in range(8) for j in range(4)]
        else:
            start = pl.multiple_of(tile * rows, rows)
            pieces = [buf[k, pl.ds(start, rows), :] for k in range(32)]
        return pieces

    def weights(buf):
        n = buf.shape[1]
        cols = [buf[:, c].reshape(NZ * 512, LANES) for c in range(n)]
        return cols[0] if n == 1 else jnp.concatenate(cols, axis=1)

    def project(buf, w, tokens_form, tile):
        pieces = operand(buf, tile, tokens_form)
        acc = jnp.dot(jnp.concatenate(pieces, axis=1), weights(w), preferred_element_type=jnp.float32)
        square = jnp.zeros((rows, LANES), jnp.float32)
        for piece in pieces:
            v = piece.astype(jnp.float32)
            square = square + v * v
        mean = jnp.sum(square, axis=1, keepdims=True) * (1.0 / (32 * LANES))
        acc = acc * lax.rsqrt(mean + 1e-06)
        start = pl.multiple_of(8 + tile * rows, 8)
        for c in range(3):
            proj[c, pl.ds(start, rows), :] = acc[:, LANES * c : LANES * (c + 1)].astype(jnp.bfloat16).astype(jnp.float32)

    def feature(block, c, start):
        out = None
        for s in range(3):
            r = 9 * block + 3 * c + s
            term = tap[r : r + 1, :] * proj[c, pl.ds(8 + start - s, rows), :]
            out = term if out is None else out + term
        return out

    def product(block, tile):
        start = tile * rows
        kv[pl.ds(SPAN + start, rows), :] = (feature(block, 1, start) * feature(block, 2, start)).astype(jnp.bfloat16)

    inside = (z > 0).astype(jnp.float32)

    def halo(block):
        a = remote(proj.at[:, pl.ds(total, 8)], rim.at[block], hsem.at[block, 0], hsem.at[block, 1], at["zp"])
        b = remote(kv.at[pl.ds(total, SPAN)], tail.at[block], hsem.at[block, 2], hsem.at[block, 3], at["zp"])
        return a, b

    def mixer(block, target):
        rim_copy, tail_copy = halo(block)
        rim_copy.start()
        product(block, 3)
        tail_copy.start()
        product(block, 2)
        product(block, 1)
        rim_copy.wait_recv()
        proj[:, pl.ds(0, 8), :] = rim[block] * inside
        product(block, 0)
        tail_copy.wait_recv()
        kv[pl.ds(0, SPAN), :] = (tail[block].astype(jnp.float32) * inside).astype(jnp.bfloat16)
        group = lax.broadcasted_iota(jnp.int32, (SPAN, LANES), 1) // 16
        for tile in range(4):
            start = tile * rows
            query = feature(block, 0, start)
            wide = jnp.concatenate([kv[pl.ds(start + SPAN * b, 2 * SPAN), :] for b in range(3)], axis=1)
            out = jnp.dot(toep[block], wide, preferred_element_type=jnp.float32)
            for b in range(3):
                inner = jnp.zeros((SPAN, LANES), jnp.float32)
                for g in range(8):
                    inner = jnp.where(group == g, out[SPAN * g : SPAN * (g + 1), LANES * b : LANES * (b + 1)], inner)
                value = (query[SPAN * b : SPAN * (b + 1)] * inner).astype(jnp.bfloat16)
                target[pl.ds(start + SPAN * b, SPAN), :] = value
        rim_copy.wait_send()
        tail_copy.wait_send()

    def give(src, out, index):
        cols = pl.ds(pl.multiple_of(y * LANES, LANES), LANES)
        dst = out.at[:, cols]
        mine = pltpu.make_async_copy(src.at[pl.ds(pl.multiple_of(y * rows, rows), rows)], dst, lsem.at[3 + index])
        mine.start()
        sent = []
        for d in (1, 3, 2):
            to = (y + d) % NY
            copy = remote(src.at[pl.ds(pl.multiple_of(to * rows, rows), rows)], dst, osem.at[index, 0, d], osem.at[index, 1, d], at["y%d" % d])
            copy.start()
            sent.append(copy)

        def finish():
            mine.wait()
            for d, copy in zip((1, 3, 2), sent):
                frm = pl.ds(pl.multiple_of(((y + NY - d) % NY) * LANES, LANES), LANES)
                ref = out.at[:, frm]
                remote(ref, ref, osem.at[index, 0, d], osem.at[index, 1, d], at["y%d" % d]).wait_recv()
                copy.wait_send()

        return finish

    steps = gx.steps()
    steps[0]()
    scale(0)
    rings[0].trade()
    rings[1].trade()
    scale(1)
    rings[2].trade()
    steps[1]()
    rs[0][0]()
    steps[2]()
    steps[3]()
    rs[0][1]()
    build(0)
    steps[4]()
    steps[5]()
    rs[0][2]()
    build(1)
    steps[6]()
    steps[7]()
    rs[0][3]()
    for run in steps[8:]:
        run()
    rs[0][4]()
    rs[1][0]()
    rs[2][0]()

    def project0(tile, carry):
        project(xbuf, w0, True, tile)
        return carry

    lax.fori_loop(0, 4, project0, 0)
    rs[1][1]()
    rs[2][1]()
    mixer(0, ybuf.at[own])
    steps = gy.steps()
    steps[0]()
    rs[1][2]()
    steps[1]()
    rs[1][3]()
    steps[2]()
    steps[3]()
    rs[1][4]()
    rs[2][2]()
    for run in steps[4:]:
        run()
    rs[2][3]()

    def outer(tile, carry):
        pieces = operand(ybuf, tile, False)
        delta = jnp.dot(jnp.concatenate(pieces, axis=1), weights(wo), preferred_element_type=jnp.float32)
        old = xbuf[mp * NY + tile, pl.ds(pl.multiple_of(y * rows, rows), rows), :]
        sbuf[own, pl.ds(pl.multiple_of(tile * rows, rows), rows), :] = (old.astype(jnp.float32) + delta).astype(jnp.bfloat16)
        return carry

    lax.fori_loop(0, 4, outer, 0)
    steps = gs.steps()
    steps[0]()
    finish_stream = give(sbuf.at[own], stream_ref, 0)
    steps[1]()
    rs[2][4]()
    for run in steps[2:]:
        run()

    def project1(tile, carry):
        project(sbuf, w1, False, tile)
        return carry

    lax.fori_loop(0, 4, project1, 0)
    mixer(1, mix)
    finish_mixed = give(mix, mixed_ref, 1)
    finish_stream()
    for g in gathers:
        g.drain()
    for r in rings:
        r.drain()
    finish_mixed()


def local(tokens, norm_gain, in_weight, feat_filter, short_filter, medium_filter, out_weight):
    rows, cols = tokens.shape
    groups = short_filter.shape[0]
    filt = jnp.stack([
        jnp.pad(f, ((0, 0), (0, 2 * SPAN - f.shape[1]))) for f in (short_filter, medium_filter)
    ])
    taps = feat_filter.reshape(-1, cols)
    total = rows * NY
    bf16, f32 = jnp.bfloat16, jnp.float32
    out = jax.ShapeDtypeStruct((rows, cols), bf16)
    any_spec = pl.BlockSpec(memory_space=pl.ANY)
    return pl.pallas_call(
        kernel,
        out_shape=(out, out),
        in_specs=[any_spec] * 6,
        out_specs=(any_spec, any_spec),
        scratch_shapes=[
            pltpu.VMEM((32, total, LANES), bf16),
            pltpu.VMEM((32, total, LANES), bf16),
            pltpu.VMEM((32, total, LANES), bf16),
            pltpu.VMEM((NZ, 3, 512, LANES), bf16),
            pltpu.VMEM((NZ, 1, 512, LANES), bf16),
            pltpu.VMEM((NZ, 3, 512, LANES), bf16),
            pltpu.VMEM((7, 128, cols), bf16),
            pltpu.VMEM((2, LANES), f32),
            pltpu.VMEM((18, LANES), f32),
            pltpu.VMEM((2, 8, 2 * SPAN), f32),
            pltpu.VMEM((2, 8 * SPAN, 2 * SPAN), bf16),
            pltpu.VMEM((3, 8 + total, LANES), f32),
            pltpu.VMEM((2, 3, 8, LANES), f32),
            pltpu.VMEM((2, SPAN, LANES), bf16),
            pltpu.VMEM((SPAN + total, LANES), bf16),
            pltpu.VMEM((total, LANES), bf16),
            pltpu.SemaphoreType.DMA((3, 4, 41)),
            pltpu.SemaphoreType.DMA((3, 2, 12)),
            pltpu.SemaphoreType.DMA((2, 4)),
            pltpu.SemaphoreType.DMA((2, 2, 4)),
            pltpu.SemaphoreType.DMA((10,)),
        ],
        compiler_params=pltpu.CompilerParams(
            collective_id=0, has_side_effects=True, vmem_limit_bytes=62 << 20
        ),
        name="hyena",
    )(tokens, norm_gain, in_weight, taps, filt, out_weight)


def solution(mesh):
    placed = (
        P("seq", "mp"),
        P(),
        P(None, None, "seq", "mp"),
        P(None, None, None, "mp"),
        P("mp", None),
        P("mp", None),
        P("seq", "mp"),
    )
    return jax.shard_map(
        local,
        mesh=mesh,
        in_specs=placed,
        out_specs=(P("seq", "mp"), P("seq", "mp")),
        check_vma=False,
    )
```

time: 598 us -> 194 us (0.32)
  waiting for transfers between devices: 398 us -> 0 us
  Pallas kernels: 0 us -> 187 us
  local copies, waits for them, and re-layouts: 132 us -> 4.83 us
  matrix products: 26.9 us -> 0 us
  between operations: 14.4 us -> 0.66 us
  starting transfers between devices: 11.7 us -> 0 us
  other arithmetic: 12.3 us -> 0.64 us
    all_gather x6 -> x0, waiting for transfers between devices: 395 us -> none  [the longest x2 239 us: project(): lax.all_gather(weights, 'seq', axis=1, tiled=True)]
    pallas_call x0 -> x1, Pallas kernels: none -> 187 us  [local(): pl.pallas_call(kernel, out_shape=(out, out), in_specs=[any_spec] * 6, out...]
    gather x4 -> x0, local copies, waits for them, and re-layouts: 121 us -> none  [the longest x2 61.2 us: toeplitz_conv(): current = jnp.where(lag >= 0, filt[:, jnp.clip(lag, 0, width - 1)], 0.0)]
    dot_general x5 -> x0, matrix products: 26.9 us -> none  [the longest x2 16.5 us: project(): jnp.einsum('rd,cdf->crf', normed, lax.all_gather(weights, 'seq', axis=1,...]
    ppermute x4 -> x0, starting transfers between devices: 11.5 us -> none  [shifted(): return lax.ppermute(x, axis, pairs)]
    slice x11 -> x0, local copies, waits for them, and re-layouts: 7.8 us -> none  [the longest x2 2.12 us: toeplitz_conv(): blocks[:-1]]
  transfers between devices with their start and end apart: 10 -> 0, of which waited for: 8 -> 0; matrix products, arithmetic and copies ran while one was open for 25% -> 0% of each run, Pallas kernels for 0% -> 0%
where the time goes in v1:
time: 194 us
  Pallas kernels  187 us (96%)
  local copies, waits for them, and re-layouts  4.83 us (2%)
    pallas_call x1, Pallas kernels, local(): pl.pallas_call(kernel, out_shape=(out, out), in_specs=[any_spec] * 6, out...  187 us
    unnamed x8, local copies, waits for them, and re-layouts  4.19 us

profile of v1, /device:TPU:1, one launch (start us, length us, event | category | flops | bytes accessed | tf_op | source)
XLA Modules:
  0.0 193.6 jit_solution(3217005112113599574)
XLA Ops:
  0.6 0.8 copy.12
  1.4 0.8 copy.11
  2.2 0.0 copy-start.1
  2.2 0.6 reshape.7.taps
  2.8 0.1 copy-done.1
  2.9 0.6 pad_maximum_fusion.filt
  3.5 187.5 %hyena.1 = (bf16[384,512]{1,0:T(8,128)(2,1)}, bf16[384,512]{1,0:T(8,128)(2,1)}) custom-call(bf16[384,512]{1,0:T(8,128)(2,1)} %tok.1, f32[2,4096]{1,0:T(2,128)} %gain.1, bf16[2,3,128,512]{3,2,1,0:T(8,128)(2,1)} %w_in.1, f32[18,512]{1,0:T(8,128)} %reshape.7.taps, f32[2,32,256]{2,1,0:T(8,128)} %pad_maximum_fusion.filt, bf16[128,512]{1,0:T(8,128)(2,1)} %w_out.1), custom_call_target="tpu_custom_call" | custom-call | tf_op jit(solution)/shard_map/hyena/pallas_call | solution.py:454
  191.0 0.0 copy-start
  191.1 1.8 copy.15
  192.9 0.0 copy-done
  192.9 0.7 copy.16
  (1 shorter events, 0.0 us)
Async XLA Ops:
  2.2 0.7 copy-start.1
  191.0 1.8 copy-start

commit v2 on v1

v2 whole, which is shorter than its diff:
```python
import jax
import jax.numpy as jnp
from jax import lax
from jax.experimental import pallas as pl
from jax.experimental.pallas import tpu as pltpu
from jax.sharding import PartitionSpec as P

NY = 4
NX = 4
NZ = 8
LANES = 128
SPAN = 128


def remote(src, dst, send_sem, recv_sem, device):
    return pltpu.make_async_remote_copy(
        src_ref=src,
        dst_ref=dst,
        send_sem=send_sem,
        recv_sem=recv_sem,
        device_id=device,
        device_id_type=pl.DeviceIdType.MESH,
    )


class Gather:
    def __init__(self, buf, start, size, part, sems, index, at):
        self.buf, self.sems, self.index, self.at = buf, sems, index, at
        self.start, self.size, self.part = start, size, part
        self.sent = []
        self.passed = []
        self.ids = {}

    def slot(self, dx, dy, core):
        at = self.at
        return (((at["x"] + dx + NX) % NX) * 2 + core) * NY + (at["y"] + dy + NY) % NY

    def sem(self, kind, key):
        return self.sems.at[self.index, kind, self.ids.setdefault(key, len(self.ids))]

    def span(self, rows):
        half = self.size // 2
        start, size = {"all": (0, 2), "lo": (0, 1), "hi": (1, 1)}[rows]
        return pl.ds(self.start + start * half, size * half)

    def place(self, off):
        return off if self.part == 0 else (off[1], off[0])

    def edge(self, step, off, rows, received):
        axis, sign = step
        key = (step, off, rows)
        if received:
            off = (off[0] - sign, off[1]) if axis == 0 else (off[0], off[1] - sign)
        ref = self.buf.at[self.slot(*self.place(off), self.at["core"]), self.span(rows)]
        physical = axis if self.part == 0 else 1 - axis
        where = self.at[("xp", "xm", "yp", "ym")[2 * physical + (0 if sign > 0 else 1)]]
        return remote(ref, ref, self.sem(0, key), self.sem(1, key), where)

    def send(self, *args):
        out = self.edge(*args, False)
        out.start()
        self.sent.append(out)

    def receive(self, *args):
        self.edge(*args, True).wait_recv()

    def hand(self, off, rows="all"):
        key = ("hand", off, rows)
        sems = self.sem(0, key), self.sem(1, key)
        core = self.at["core"]
        here = self.buf.at[self.slot(*self.place(off), core), self.span(rows)]
        out = remote(here, here, *sems, self.at["cp"])
        out.start()
        self.passed.append((out, off, rows, sems))

    def steps(self):
        first_axis, second_axis = ((0, 1), (0, -1)), ((1, 1), (1, -1))

        def piece(sign):
            return "lo" if sign > 0 else "hi"

        def begin():
            for step in first_axis + second_axis:
                self.send(step, (0, 0), "all")
            self.hand((0, 0))

        def first():
            for sign in (1, -1):
                self.receive((0, sign), (0, 0), "all")
                self.send((0, sign), (-sign, 0), piece(sign))
                for step in second_axis:
                    self.send(step, (-sign, 0), "all")
                self.hand((-sign, 0))

        def across(a):
            def run():
                for sign in (1, -1):
                    self.receive((1, sign), (a, 0), "all")
                    self.send((1, sign), (a, -sign), piece(sign))
                    self.hand((a, -sign))
            return run

        def far():
            for sign in (1, -1):
                self.receive((0, sign), (-sign, 0), piece(sign))
            for step in second_axis:
                self.send(step, (2, 0), "all")
            self.hand((2, 0))

        def last(a):
            def run():
                for sign in (1, -1):
                    self.receive((1, sign), (a, -sign), piece(sign))
                self.hand((a, 2))
            return run

        def end():
            for _, off, rows, sems in self.passed:
                twin = self.buf.at[self.slot(*self.place(off), 1 - self.at["core"]), self.span(rows)]
                remote(twin, twin, *sems, self.at["cp"]).wait_recv()

        return [begin, first, across(0), far, across(-1), across(1), last(0), across(2), last(-1), last(1), last(2), end]

    def drain(self):
        for out in self.sent:
            out.wait_send()
        for item in self.passed:
            item[0].wait_send()


class Ring:
    def __init__(self, buf, stage, first, lump, sems, index, at, local_sem):
        self.lump = lump
        self.buf, self.sems, self.index, self.at = buf, sems, index, at
        self.stage, self.first, self.local_sem = stage, first, local_sem
        self.sent = []
        self.count = buf.shape[1]

    def trade(self):
        at = self.at
        rows = pl.ds(at["y"] * LANES, LANES)
        dst = self.buf.at[at["z"], :, rows]
        part = pl.ds(self.first, self.count)
        self.mine = pltpu.make_async_copy(
            self.stage.at[part, :, pl.ds(pl.multiple_of(at["y"] * LANES, LANES), LANES)], dst, self.local_sem
        )
        self.mine.start()
        for d in (1, 3, 2):
            to = (at["y"] + d) % NY
            src = self.stage.at[part, :, pl.ds(pl.multiple_of(to * LANES, LANES), LANES)]
            out = remote(src, dst, self.sems.at[self.index, 0, d], self.sems.at[self.index, 1, d], at["y%d" % d])
            out.start()
            self.sent.append(out)

    def copy(self, sign, s, c, received):
        off = -sign * (s + (1 if received else 0))
        ref = self.buf.at[(self.at["z"] + off + NZ) % NZ, pl.ds(c * self.lump, self.lump)]
        half = ref.shape[1] // 2
        if s == 3:
            ref = ref.at[:, pl.ds(0 if sign > 0 else half, half)]
        k = 4 + 8 * c + (0 if sign > 0 else 4) + s
        return remote(ref, ref, self.sems.at[self.index, 0, k], self.sems.at[self.index, 1, k], self.at["zp" if sign > 0 else "zm"])

    def send(self, sign, s, c):
        out = self.copy(sign, s, c, False)
        out.start()
        self.sent.append(out)

    def steps(self):
        lumps = range(self.count // self.lump)

        def begin():
            at = self.at
            self.mine.wait()
            for d in (1, 3, 2):
                rows = pl.ds(((at["y"] + NY - d) % NY) * LANES, LANES)
                ref = self.buf.at[at["z"], :, rows]
                remote(ref, ref, self.sems.at[self.index, 0, d], self.sems.at[self.index, 1, d], at["y%d" % d]).wait_recv()
            for c in lumps:
                self.send(1, 0, c)
                self.send(-1, 0, c)

        def step(s):
            def run():
                for c in lumps:
                    for sign in (1, -1):
                        self.copy(sign, s - 1, c, True).wait_recv()
                        if s < 4:
                            self.send(sign, s, c)
            return run

        return [begin] + [step(s) for s in (1, 2, 3, 4)]

    def drain(self):
        for out in self.sent:
            out.wait_send()


def kernel(tok, gain, w_in, taps, filt, w_out, stream_ref, mixed_ref,
           xbuf, ybuf, sbuf, w0, wo, w1, stage, gcol, tap, fil, toep, proj, rim, tail, kv, mix,
           gsem, wsem, hsem, osem, lsem):
    seq = lax.axis_index("seq")
    mp = lax.axis_index("mp")
    y, z = seq % NY, seq // NY
    x, core = mp // 2, mp % 2
    at = {"x": x, "y": y, "z": z, "core": core}
    at["xp"] = {"mp": ((x + 1) % NX) * 2 + core}
    at["xm"] = {"mp": ((x + NX - 1) % NX) * 2 + core}
    at["cp"] = {"mp": x * 2 + 1 - core}
    for d in (1, 2, 3):
        at["y%d" % d] = {"seq": z * NY + (y + d) % NY}
    at["yp"], at["ym"] = at["y1"], at["y3"]
    at["zp"] = {"seq": ((z + 1) % NZ) * NY + y}
    at["zm"] = {"seq": ((z + NZ - 1) % NZ) * NY + y}
    own = mp * NY + y
    rows = tok.shape[0]
    total = rows * NY

    loads = [
        pltpu.make_async_copy(tok.at[:, pl.ds(LANES * i, LANES)], xbuf.at[own, pl.ds(rows * i, rows)], lsem.at[i])
        for i in range(4)
    ]
    loads.append(pltpu.make_async_copy(w_in.at[0], stage.at[pl.ds(0, 3)], lsem.at[4]))
    loads.append(pltpu.make_async_copy(w_out, stage.at[3], lsem.at[5]))
    loads.append(pltpu.make_async_copy(w_in.at[1], stage.at[pl.ds(4, 3)], lsem.at[6]))
    loads.append(pltpu.make_async_copy(gain.at[:, pl.ds(pl.multiple_of(seq * LANES, LANES), LANES)], gcol, lsem.at[7]))
    loads.append(pltpu.make_async_copy(taps.at[:, pl.ds(pl.multiple_of(y * LANES, LANES), LANES)], tap, lsem.at[8]))
    loads.append(pltpu.make_async_copy(filt.at[:, pl.ds(pl.multiple_of(y * 8, 8), 8)], fil, lsem.at[9]))
    for c in loads:
        c.start()

    barrier = pltpu.get_barrier_semaphore()
    peers = ("xp", "xm", "cp", "y1", "y2", "y3", "zp", "zm")
    for name in peers:
        pl.semaphore_signal(barrier, inc=1, device_id=at[name], device_id_type=pl.DeviceIdType.MESH)
    half = total // 2
    token_streams = [Gather(xbuf, half * i, half, i, gsem, i, at) for i in range(2)]
    mix_streams = [Gather(ybuf, rows * i, rows, i % 2, gsem, 2 + i, at) for i in range(4)]
    next_streams = [Gather(sbuf, rows * i, rows, i % 2, gsem, 6 + i, at) for i in range(4)]

    rings = [
        Ring(w0, stage, 0, 1, wsem, 0, at, lsem.at[0]),
        Ring(wo, stage, 3, 1, wsem, 1, at, lsem.at[1]),
        Ring(w1, stage, 4, 3, wsem, 2, at, lsem.at[2]),
    ]
    rs = [r.steps() for r in rings]

    def scale(block):
        column = jnp.transpose(jnp.broadcast_to(gcol[block : block + 1, :], (LANES, LANES)))
        for c in range(3):
            for j in range(4):
                lanes = pl.ds(LANES * j, LANES)
                value = stage[4 * block + c, :, lanes].astype(jnp.float32) * column
                stage[4 * block + c, :, lanes] = value.astype(jnp.bfloat16)

    def build(block):
        for g in range(8):
            line = jnp.broadcast_to(fil[block, g : g + 1, :], (2 * SPAN, 2 * SPAN))
            skew = pltpu.roll(line, SPAN, 1, stride=1, stride_axis=0)
            toep[block, pl.ds(SPAN * g, SPAN), :] = jnp.transpose(skew[:, :SPAN]).astype(jnp.bfloat16)

    def operand(buf, tile, tokens_form):
        if tokens_form:
            pieces = [buf[m * NY + tile, pl.ds(rows * j, rows), :] for m in range(8) for j in range(4)]
        else:
            start = pl.multiple_of(tile * rows, rows)
            pieces = [buf[k, pl.ds(start, rows), :] for k in range(32)]
        return pieces

    def weights(buf):
        n = buf.shape[1]
        cols = [buf[:, c].reshape(NZ * 512, LANES) for c in range(n)]
        return cols[0] if n == 1 else jnp.concatenate(cols, axis=1)

    def project(buf, w, tokens_form, tile):
        pieces = operand(buf, tile, tokens_form)
        acc = jnp.dot(jnp.concatenate(pieces, axis=1), weights(w), preferred_element_type=jnp.float32)
        square = jnp.zeros((rows, LANES), jnp.float32)
        for piece in pieces:
            v = piece.astype(jnp.float32)
            square = square + v * v
        mean = jnp.sum(square, axis=1, keepdims=True) * (1.0 / (32 * LANES))
        acc = acc * lax.rsqrt(mean + 1e-06)
        start = pl.multiple_of(8 + tile * rows, 8)
        for c in range(3):
            proj[c, pl.ds(start, rows), :] = acc[:, LANES * c : LANES * (c + 1)].astype(jnp.bfloat16).astype(jnp.float32)

    def feature(block, c, start, count):
        out = None
        for s in range(3):
            r = 9 * block + 3 * c + s
            term = tap[r : r + 1, :] * proj[c, pl.ds(8 + start - s, count), :]
            out = term if out is None else out + term
        return out

    def product(block, start, count):
        value = feature(block, 1, start, count) * feature(block, 2, start, count)
        kv[pl.ds(SPAN + start, count), :] = value.astype(jnp.bfloat16)

    def product_head(block, tile):
        product(block, tile * rows, 16)

    def product_rest(block, tile):
        product(block, tile * rows + 16, rows - 16)

    inside = (z > 0).astype(jnp.float32)

    def halo(block):
        a = remote(proj.at[:, pl.ds(total, 8)], rim.at[block], hsem.at[block, 0], hsem.at[block, 1], at["zp"])
        b = remote(kv.at[pl.ds(total, SPAN)], tail.at[block], hsem.at[block, 2], hsem.at[block, 3], at["zp"])
        return a, b

    group = lax.broadcasted_iota(jnp.int32, (SPAN, LANES), 1) // 16

    def conv(block, tile, target):
        start = tile * rows
        query = feature(block, 0, start, rows)
        wide = jnp.concatenate([kv[pl.ds(start + SPAN * b, 2 * SPAN), :] for b in range(3)], axis=1)
        out = jnp.dot(toep[block], wide, preferred_element_type=jnp.float32)
        for b in range(3):
            inner = jnp.zeros((SPAN, LANES), jnp.float32)
            for g in range(8):
                inner = jnp.where(group == g, out[SPAN * g : SPAN * (g + 1), LANES * b : LANES * (b + 1)], inner)
            value = (query[SPAN * b : SPAN * (b + 1)] * inner).astype(jnp.bfloat16)
            target[pl.ds(start + SPAN * b, SPAN), :] = value

    def take_rim(block, copy):
        copy.wait_recv()
        proj[:, pl.ds(0, 8), :] = rim[block] * inside

    def take_tail(block, copy):
        copy.wait_recv()
        kv[pl.ds(0, SPAN), :] = (tail[block].astype(jnp.float32) * inside).astype(jnp.bfloat16)

    def give(src, out, index, tile):
        d = (tile - y + NY) % NY
        part = src.at[pl.ds(tile * rows, rows)]
        dst = out.at[:, pl.ds(pl.multiple_of(y * LANES, LANES), LANES)]

        @pl.when(d == 0)
        def _():
            pltpu.make_async_copy(part, dst, lsem.at[3 + index]).start()

        @pl.when(d != 0)
        def _():
            remote(part, dst, osem.at[index, 0, d], osem.at[index, 1, d], {"seq": z * NY + tile}).start()

    def given(src, out, index):
        part = src.at[pl.ds(pl.multiple_of(y * rows, rows), rows)]
        cols = [out.at[:, pl.ds(pl.multiple_of(((y + NY - d) % NY) * LANES, LANES), LANES)] for d in range(NY)]
        pltpu.make_async_copy(part, cols[0], lsem.at[3 + index]).wait()
        for d in (1, 3, 2):
            copy = remote(part, cols[d], osem.at[index, 0, d], osem.at[index, 1, d], at["y%d" % d])
            copy.wait_recv()
            copy.wait_send()

    def outer(tile):
        delta = jnp.dot(jnp.concatenate(operand(ybuf, tile, False), axis=1), weights(wo), preferred_element_type=jnp.float32)
        old = xbuf[mp * NY + tile, pl.ds(pl.multiple_of(y * rows, rows), rows), :]
        sbuf[own, pl.ds(tile * rows, rows), :] = (old.astype(jnp.float32) + delta).astype(jnp.bfloat16)

    def pair(streams):
        p, q = (stream.steps() for stream in streams)

        def both(i):
            def run():
                p[i]()
                q[i]()
            return run

        return p, q, [both(i) for i in range(len(p))]

    for c in loads[4:]:
        c.wait()
    scale(0)
    for c in loads[:4]:
        c.wait()
    pl.semaphore_wait(barrier, len(peers))

    rings[0].trade()
    _, _, tk = pair(token_streams)
    tk[0]()
    scale(1)
    build(0)
    tk[1]()
    rs[0][0]()
    tk[2]()
    tk[3]()
    rs[0][1]()
    tk[4]()
    tk[5]()
    rs[0][2]()
    build(1)
    tk[6]()
    tk[7]()
    rs[0][3]()
    for run in tk[8:]:
        run()
    rings[1].trade()
    rings[2].trade()
    rs[0][4]()

    first_out = ybuf.at[own]
    rim_copy, tail_copy = halo(0)
    y0, y1, ya = pair(mix_streams[:2])
    y2, y3, yb = pair(mix_streams[2:])
    s0, s1, sa = pair(next_streams[:2])
    s2, s3, sb = pair(next_streams[2:])
    project(xbuf, w0, True, 3)
    rim_copy.start()
    product_rest(0, 3)
    tail_copy.start()
    rs[1][0]()
    rs[2][0]()
    project(xbuf, w0, True, 0)
    take_rim(0, rim_copy)
    product(0, 0, rows)
    take_tail(0, tail_copy)
    conv(0, 0, first_out)
    y0[0]()
    project(xbuf, w0, True, 1)
    product(0, rows, rows)
    conv(0, 1, first_out)
    y1[0]()
    rs[1][1]()
    y0[1]()
    project(xbuf, w0, True, 2)
    product(0, 2 * rows, rows + 16)
    conv(0, 2, first_out)
    y2[0]()
    y1[1]()
    conv(0, 3, first_out)
    y3[0]()
    rim_copy.wait_send()
    tail_copy.wait_send()
    rs[1][2]()
    ya[2]()
    ya[3]()
    rs[1][3]()
    rs[2][1]()
    ya[4]()
    ya[5]()
    yb[1]()
    rs[1][4]()
    ya[6]()
    yb[2]()
    ya[7]()
    yb[3]()
    ya[8]()
    yb[4]()
    ya[9]()
    yb[5]()
    ya[10]()
    yb[6]()
    rs[2][2]()
    ya[11]()

    for tile, begin in ((0, s0), (1, s1)):
        outer(tile)
        begin[0]()
    yb[7]()
    sa[1]()
    yb[8]()
    sa[2]()
    yb[9]()
    sa[3]()
    yb[10]()
    sa[4]()
    rs[2][3]()
    yb[11]()
    for tile, begin in ((2, s2), (3, s3)):
        outer(tile)
        begin[0]()
    for tile in range(4):
        give(sbuf.at[own], stream_ref, 0, tile)
    sa[5]()
    sa[6]()
    sb[1]()
    sa[7]()
    sb[2]()
    sa[8]()
    sb[3]()
    sa[9]()
    sb[4]()
    rs[2][4]()
    sa[10]()
    sb[5]()
    sa[11]()
    project(sbuf, w1, False, 0)
    sb[6]()
    sb[7]()
    project(sbuf, w1, False, 1)
    sb[8]()
    sb[9]()
    product_rest(1, 0)
    product(1, rows, rows)
    sb[10]()
    conv(1, 1, mix)
    give(mix, mixed_ref, 1, 1)
    sb[11]()
    rim_copy, tail_copy = halo(1)
    project(sbuf, w1, False, 3)
    rim_copy.start()
    product_rest(1, 3)
    tail_copy.start()
    project(sbuf, w1, False, 2)
    product(1, 2 * rows, rows + 16)
    conv(1, 3, mix)
    give(mix, mixed_ref, 1, 3)
    conv(1, 2, mix)
    give(mix, mixed_ref, 1, 2)
    take_rim(1, rim_copy)
    product_head(1, 0)
    take_tail(1, tail_copy)
    conv(1, 0, mix)
    give(mix, mixed_ref, 1, 0)
    given(sbuf.at[own], stream_ref, 0)
    rim_copy.wait_send()
    tail_copy.wait_send()
    for stream in token_streams + mix_streams + next_streams:
        stream.drain()
    for r in rings:
        r.drain()
    given(mix, mixed_ref, 1)


def local(tokens, norm_gain, in_weight, feat_filter, short_filter, medium_filter, out_weight):
    rows, cols = tokens.shape
    groups = short_filter.shape[0]
    filt = jnp.stack([
        jnp.pad(f, ((0, 0), (0, 2 * SPAN - f.shape[1]))) for f in (short_filter, medium_filter)
    ])
    taps = feat_filter.reshape(-1, cols)
    total = rows * NY
    bf16, f32 = jnp.bfloat16, jnp.float32
    out = jax.ShapeDtypeStruct((rows, cols), bf16)
    any_spec = pl.BlockSpec(memory_space=pl.ANY)
    return pl.pallas_call(
        kernel,
        out_shape=(out, out),
        in_specs=[any_spec] * 6,
        out_specs=(any_spec, any_spec),
        scratch_shapes=[
            pltpu.VMEM((32, total, LANES), bf16),
            pltpu.VMEM((32, total, LANES), bf16),
            pltpu.VMEM((32, total, LANES), bf16),
            pltpu.VMEM((NZ, 3, 512, LANES), bf16),
            pltpu.VMEM((NZ, 1, 512, LANES), bf16),
            pltpu.VMEM((NZ, 3, 512, LANES), bf16),
            pltpu.VMEM((7, 128, cols), bf16),
            pltpu.VMEM((2, LANES), f32),
            pltpu.VMEM((18, LANES), f32),
            pltpu.VMEM((2, 8, 2 * SPAN), f32),
            pltpu.VMEM((2, 8 * SPAN, 2 * SPAN), bf16),
            pltpu.VMEM((3, 8 + total, LANES), f32),
            pltpu.VMEM((2, 3, 8, LANES), f32),
            pltpu.VMEM((2, SPAN, LANES), bf16),
            pltpu.VMEM((SPAN + total, LANES), bf16),
            pltpu.VMEM((total, LANES), bf16),
            pltpu.SemaphoreType.DMA((10, 2, 36)),
            pltpu.SemaphoreType.DMA((3, 2, 28)),
            pltpu.SemaphoreType.DMA((2, 4)),
            pltpu.SemaphoreType.DMA((2, 2, 4)),
            pltpu.SemaphoreType.DMA((10,)),
        ],
        compiler_params=pltpu.CompilerParams(
            collective_id=0, has_side_effects=True, vmem_limit_bytes=62 << 20
        ),
        name="hyena",
    )(tokens, norm_gain, in_weight, taps, filt, out_weight)


def solution(mesh):
    placed = (
        P("seq", "mp"),
        P(),
        P(None, None, "seq", "mp"),
        P(None, None, None, "mp"),
        P("mp", None),
        P("mp", None),
        P("seq", "mp"),
    )
    return jax.shard_map(
        local,
        mesh=mesh,
        in_specs=placed,
        out_specs=(P("seq", "mp"), P("seq", "mp")),
        check_vma=False,
    )
```

time: 194 us -> 168 us (0.87)
  Pallas kernels: 187 us -> 161 us
    pallas_call x1, Pallas kernels: 187 us -> 161 us  [local(): pl.pallas_call(kernel, out_shape=(out, out), in_specs=[any_spec] * 6, out...]
where the time goes in v2:
time: 168 us
  Pallas kernels  161 us (96%)
  local copies, waits for them, and re-layouts  4.83 us (3%)
    pallas_call x1, Pallas kernels, local(): pl.pallas_call(kernel, out_shape=(out, out), in_specs=[any_spec] * 6, out...  161 us
    unnamed x8, local copies, waits for them, and re-layouts  4.19 us

profile of v2, /device:TPU:1, one launch (start us, length us, event | category | flops | bytes accessed | tf_op | source)
XLA Modules:
  0.0 167.6 jit_solution(18069322832402171382)
XLA Ops:
  0.6 0.8 copy.12
  1.4 0.8 copy.11
  2.2 0.0 copy-start.1
  2.2 0.6 reshape.7.taps
  2.8 0.1 copy-done.1
  2.9 0.6 pad_maximum_fusion.filt
  3.5 161.4 %hyena.1 = (bf16[384,512]{1,0:T(8,128)(2,1)}, bf16[384,512]{1,0:T(8,128)(2,1)}) custom-call(bf16[384,512]{1,0:T(8,128)(2,1)} %tok.1, f32[2,4096]{1,0:T(2,128)} %gain.1, bf16[2,3,128,512]{3,2,1,0:T(8,128)(2,1)} %w_in.1, f32[18,512]{1,0:T(8,128)} %reshape.7.taps, f32[2,32,256]{2,1,0:T(8,128)} %pad_maximum_fusion.filt, bf16[128,512]{1,0:T(8,128)(2,1)} %w_out.1), custom_call_target="tpu_custom_call" | custom-call | tf_op jit(solution)/shard_map/hyena/pallas_call | solution.py:538
  165.0 0.0 copy-start
  165.0 1.8 %copy.15 = bf16[384,512]{1,0:T(8,128)(2,1)} copy(bf16[384,512]{1,0:T(8,128)(2,1)} %get-tuple-element.6) | data formatting | bytes 786432
  166.8 0.0 copy-done
  166.8 0.7 copy.16
  (1 shorter events, 0.0 us)
Async XLA Ops:
  2.2 0.7 copy-start.1
  165.0 1.8 %copy-start = (bf16[384,512]{1,0:T(8,128)(2,1)S(1)}, bf16[384,512]{1,0:T(8,128)(2,1)}, u32[]{:S(2)}) copy-start(bf16[384,512]{1,0:T(8,128)(2,1)} %get-tuple-element.7) | copy-start | bytes 1179652

commit v3 on v2

v3 whole, which is shorter than its diff:
```python
import jax
import jax.numpy as jnp
from jax import lax
from jax.experimental import pallas as pl
from jax.experimental.pallas import tpu as pltpu
from jax.sharding import PartitionSpec as P

NY = 4
NX = 4
NZ = 8
LANES = 128
SPAN = 128


def remote(src, dst, send_sem, recv_sem, device):
    return pltpu.make_async_remote_copy(
        src_ref=src,
        dst_ref=dst,
        send_sem=send_sem,
        recv_sem=recv_sem,
        device_id=device,
        device_id_type=pl.DeviceIdType.MESH,
    )


class Gather:
    def __init__(self, buf, start, size, part, sems, index, at, flat=False):
        self.flat = flat
        self.buf, self.sems, self.index, self.at = buf, sems, index, at
        self.start, self.size, self.part = start, size, part
        self.ids = {}

    def slot(self, dx, dy, core):
        at = self.at
        column = ((at["x"] + dx + NX) % NX) * 2 + core
        return column if self.flat else column * NY + (at["y"] + dy + NY) % NY

    def sem(self, kind, key):
        ids = self.ids.setdefault(kind, {})
        return self.sems.at[self.index, kind, ids.setdefault(key, len(ids))]

    def span(self, rows):
        half = self.size // 2
        start, size = {"all": (0, 2), "lo": (0, 1), "hi": (1, 1)}[rows]
        return pl.ds(self.start + start * half, size * half)

    def place(self, off):
        return off if self.part == 0 else (off[1], off[0])

    def edge(self, step, off, rows, received):
        axis, sign = step
        key = (step, off) if rows == "all" else ("pair", axis, axis * off[0])
        if received:
            off = (off[0] - sign, off[1]) if axis == 0 else (off[0], off[1] - sign)
            rows = "all"
        ref = self.buf.at[self.slot(*self.place(off), self.at["core"]), self.span(rows)]
        physical = axis if self.part == 0 else 1 - axis
        where = self.at[("xp", "xm", "yp", "ym")[2 * physical + (0 if sign > 0 else 1)]]
        return remote(ref, ref, self.sem(0, "sent"), self.sem(1, key), where)

    def send(self, *args):
        self.edge(*args, False).start()

    def receive(self, *args):
        self.edge(*args, True).wait_recv()

    def handing(self, ref):
        return remote(ref, ref, self.sem(0, "hand"), self.sem(1, "hand"), self.at["cp"])

    def hand(self, off):
        self.handing(self.buf.at[self.slot(*self.place(off), self.at["core"]), self.span("all")]).start()

    def hand_column(self, a):
        if self.part == 0:
            at = self.at
            column = ((at["x"] + a + NX) % NX) * 2 + at["core"]
            self.handing(self.buf.at[pl.ds(column * NY, NY), self.span("all")]).start()

    def hand_now(self, off):
        if self.part == 1 or self.flat:
            self.hand(off)

    def steps(self):
        first_axis, second_axis = ((0, 1), (0, -1)), () if self.flat else ((1, 1), (1, -1))

        def piece(sign):
            return "lo" if sign > 0 else "hi"

        def begin():
            for step in first_axis + second_axis:
                self.send(step, (0, 0), "all")
            self.hand_now((0, 0))

        def first():
            for sign in (1, -1):
                self.receive((0, sign), (0, 0), "all")
                self.send((0, sign), (-sign, 0), piece(sign))
                for step in second_axis:
                    self.send(step, (-sign, 0), "all")
                self.hand_now((-sign, 0))

        def across(a):
            def run():
                for sign in (1, -1):
                    self.receive((1, sign), (a, 0), "all")
                    self.send((1, sign), (a, -sign), piece(sign))
                    self.hand_now((a, -sign))
            return run

        def far():
            self.receive((0, 1), (-1, 0), "lo")
            for step in second_axis:
                self.send(step, (2, 0), "all")
            self.hand_now((2, 0))

        def last(a):
            def run():
                self.receive((1, 1), (a, -1), "lo")
                self.hand_now((a, 2))
                self.hand_column(a)
            return run

        def end():
            self.handing(self.blocks(1)).wait_recv()

        if self.flat:
            return [begin, first, far, end]
        return [begin, first, across(0), far, across(-1), across(1), last(0), across(2), last(-1), last(1), last(2), end]

    def blocks(self, extra):
        return self.buf.at[pl.ds(0, (3 if self.flat else 15) + extra), self.span("all")]

    def drain(self):
        ref = self.blocks(0)
        remote(ref, ref, self.sem(0, "sent"), self.sem(1, "hand"), self.at["xp"]).wait_send()
        self.handing(self.blocks(1)).wait_send()


class Ring:
    def __init__(self, buf, stage, first, lump, sems, index, at, local_sem):
        self.lump, self.whole = lump, False
        self.buf, self.sems, self.index, self.at = buf, sems, index, at
        self.stage, self.first, self.local_sem = stage, first, local_sem
        self.count = buf.shape[1]

    def trade(self):
        at = self.at
        rows = pl.ds(at["y"] * LANES, LANES)
        dst = self.buf.at[at["z"], :, rows]
        part = pl.ds(self.first, self.count)
        self.mine = pltpu.make_async_copy(
            self.stage.at[part, :, pl.ds(pl.multiple_of(at["y"] * LANES, LANES), LANES)], dst, self.local_sem
        )
        self.mine.start()
        for d in (1, 3, 2):
            to = (at["y"] + d) % NY
            src = self.stage.at[part, :, pl.ds(pl.multiple_of(to * LANES, LANES), LANES)]
            remote(src, dst, self.sems.at[self.index, 0, 0], self.sems.at[self.index, 1, 0], at["y%d" % d]).start()

    def traded(self):
        ref = self.buf.at[0, :, pl.ds(0, 3 * LANES)]
        return remote(ref, ref, self.sems.at[self.index, 0, 0], self.sems.at[self.index, 1, 0], self.at["y1"])

    def keep(self):
        self.whole = True
        self.mine = pltpu.make_async_copy(self.stage.at[self.first], self.buf.at[self.at["z"], 0], self.local_sem)
        self.mine.start()

    def copy(self, sign, s, c, received):
        off = -sign * (s + (1 if received else 0))
        ref = self.buf.at[(self.at["z"] + off + NZ) % NZ, pl.ds(c * self.lump, self.lump)]
        half = ref.shape[1] // 2
        if s == 3:
            ref = ref.at[:, pl.ds(0 if sign > 0 else half, half)]
        k = 4 + 8 * c + (0 if sign > 0 else 4) + s
        return remote(ref, ref, self.sems.at[self.index, 0, 1], self.sems.at[self.index, 1, k], self.at["zp" if sign > 0 else "zm"])

    def send(self, sign, s, c):
        self.copy(sign, s, c, False).start()

    def steps(self):
        lumps = range(self.count // self.lump)

        def begin():
            at = self.at
            self.mine.wait()
            if not self.whole:
                self.traded().wait_recv()
            for c in lumps:
                self.send(1, 0, c)
                self.send(-1, 0, c)

        def step(s):
            def run():
                for c in lumps:
                    for sign in (1, -1):
                        self.copy(sign, s - 1, c, True).wait_recv()
                        if s < 4:
                            self.send(sign, s, c)
            return run

        return [begin] + [step(s) for s in (1, 2, 3, 4)]

    def drain(self):
        ref = self.buf.at[pl.ds(0, NZ - 1)]
        remote(ref, ref, self.sems.at[self.index, 0, 1], self.sems.at[self.index, 1, 1], self.at["zp"]).wait_send()
        if not self.whole:
            self.traded().wait_send()


def kernel(tok, gain, w_in, taps, short, medium, w_out, stream_ref, mixed_ref,
           xbuf, ybuf, sbuf, w0, wo, w1, stage, gcol, tap, few, square, fil, toep, proj, rim, tail, kv, mix, scaler, part, relayed, summed,
           gsem, wsem, hsem, osem, dsem, lsem):
    seq = lax.axis_index("seq")
    mp = lax.axis_index("mp")
    y, z = seq % NY, seq // NY
    x, core = mp // 2, mp % 2
    at = {"x": x, "y": y, "z": z, "core": core}
    at["xp"] = {"mp": ((x + 1) % NX) * 2 + core}
    at["xm"] = {"mp": ((x + NX - 1) % NX) * 2 + core}
    at["cp"] = {"mp": x * 2 + 1 - core}
    for d in (1, 2, 3):
        at["y%d" % d] = {"seq": z * NY + (y + d) % NY}
    at["yp"], at["ym"] = at["y1"], at["y3"]
    at["zp"] = {"seq": ((z + 1) % NZ) * NY + y}
    at["zm"] = {"seq": ((z + NZ - 1) % NZ) * NY + y}
    own = mp * NY + y
    rows = tok.shape[0]
    total = rows * NY

    loads = [
        pltpu.make_async_copy(tok.at[:, pl.ds(LANES * i, LANES)], xbuf.at[own, pl.ds(rows * i, rows)], lsem.at[i])
        for i in range(4)
    ]
    loads.append(pltpu.make_async_copy(w_in.at[0], stage.at[pl.ds(0, 3)], lsem.at[4]))
    loads.append(pltpu.make_async_copy(w_out, stage.at[3], lsem.at[5]))
    loads.append(pltpu.make_async_copy(w_in.at[1], stage.at[pl.ds(4, 3)], lsem.at[6]))
    loads.append(pltpu.make_async_copy(gain.at[:, pl.ds(pl.multiple_of(seq * LANES, LANES), LANES)], gcol, lsem.at[7]))
    loads.append(pltpu.make_async_copy(taps.at[:, :, :, pl.ds(pl.multiple_of(y * LANES, LANES), LANES)], tap, lsem.at[8]))
    loads.append(pltpu.make_async_copy(medium.at[pl.ds(pl.multiple_of(y * 8, 8), 8)], fil.at[1], lsem.at[9]))
    loads.append(pltpu.make_async_copy(short, few, lsem.at[10]))
    for c in loads:
        c.start()

    barrier = pltpu.get_barrier_semaphore()
    peers = ("xp", "xm", "cp", "y1", "y2", "y3", "zp", "zm")
    for name in peers:
        pl.semaphore_signal(barrier, inc=1, device_id=at[name], device_id_type=pl.DeviceIdType.MESH)
    half = total // 2
    token_streams = [Gather(xbuf, half * i, half, i, gsem, i, at) for i in range(2)]
    mix_streams = [Gather(ybuf, rows * i, rows, 0, gsem, 2 + i, at, True) for i in range(4)]
    next_streams = [Gather(sbuf, rows * i, rows, i % 2, gsem, 6 + i, at) for i in range(4)]

    rings = [
        Ring(w0, stage, 0, 1, wsem, 0, at, lsem.at[0]),
        Ring(wo, stage, 3, 1, wsem, 1, at, lsem.at[1]),
        Ring(w1, stage, 4, 3, wsem, 2, at, lsem.at[2]),
    ]
    rs = [r.steps() for r in rings]

    def scale(block):
        column = jnp.transpose(jnp.broadcast_to(gcol[block : block + 1, :], (LANES, LANES)))
        for c in range(3):
            for j in range(4):
                lanes = pl.ds(LANES * j, LANES)
                value = stage[4 * block + c, :, lanes].astype(jnp.float32) * column
                stage[4 * block + c, :, lanes] = value.astype(jnp.bfloat16)

    def spread():
        square[...] = jnp.zeros_like(square)
        square[0 : few.shape[0], 0 : few.shape[1]] = few[...]
        square[...] = jnp.transpose(square[...])
        fil[0] = square[pl.ds(pl.multiple_of(y * 8, 8), 8), :]

    def build(block):
        for g in range(8):
            taps_here = jnp.broadcast_to(fil[block, g : g + 1, :], (2 * SPAN, SPAN))
            line = jnp.concatenate([taps_here, jnp.zeros_like(taps_here)], axis=1)
            skew = pltpu.roll(line, SPAN, 1, stride=1, stride_axis=0)
            toep[block, pl.ds(SPAN * g, SPAN), :] = jnp.transpose(skew[:, :SPAN]).astype(jnp.bfloat16)

    def operand(buf, tile, tokens_form):
        if tokens_form:
            pieces = [buf[m * NY + tile, pl.ds(rows * j, rows), :] for m in range(8) for j in range(4)]
        else:
            start = pl.multiple_of(tile * rows, rows)
            pieces = [buf[k, pl.ds(start, rows), :] for k in range(32)]
        return pieces

    def weights(buf):
        n = buf.shape[1]
        cols = [buf[:, c].reshape(NZ * 512, LANES) for c in range(n)]
        return cols[0] if n == 1 else jnp.concatenate(cols, axis=1)

    def scale_rows(pieces):
        square = jnp.zeros((rows, LANES), jnp.float32)
        for piece in pieces:
            v = piece.astype(jnp.float32)
            square = square + v * v
        mean = jnp.sum(square, axis=1, keepdims=True) * (1.0 / (32 * LANES))
        return lax.rsqrt(mean + 1e-06)

    def store(acc, tile):
        start = pl.multiple_of(8 + tile * rows, 8)
        for c in range(3):
            value = acc[:, LANES * c : LANES * (c + 1)].astype(jnp.bfloat16)
            proj[c, pl.ds(start, rows), :] = value.astype(jnp.float32)

    def project(tile):
        pieces = operand(sbuf, tile, False)
        acc = jnp.dot(jnp.concatenate(pieces, axis=1), weights(w1), preferred_element_type=jnp.float32)
        store(acc * scale_rows(pieces), tile)

    def some(tile, offs):
        left, right = [], []
        for off in offs:
            k = (z + off) % NZ
            left += [xbuf[k * NY + tile, pl.ds(rows * j, rows), :] for j in range(4)]
            right.append(jnp.concatenate([w0[k, c] for c in range(3)], axis=1))
        return jnp.dot(
            jnp.concatenate(left, axis=1), jnp.concatenate(right, axis=0), preferred_element_type=jnp.float32
        )

    def project_near(tile, carry):
        acc = some(tile, (0, 1, 7, 2, 6))
        start = pl.multiple_of(8 + tile * rows, 8)
        for c in range(3):
            proj[c, pl.ds(start, rows), :] = acc[:, LANES * c : LANES * (c + 1)]
        scaler[pl.ds(pl.multiple_of(tile * rows, rows), rows), :] = jnp.broadcast_to(
            scale_rows(operand(xbuf, tile, True)), (rows, LANES)
        )
        return carry

    def project_far(tile):
        acc = some(tile, (3, 5, 4))
        near = jnp.concatenate([proj[c, pl.ds(8 + tile * rows, rows), :] for c in range(3)], axis=1)
        factor = scaler[pl.ds(tile * rows, rows), :]
        store((acc + near) * jnp.concatenate([factor] * 3, axis=1), tile)

    def feature(block, c, start, count):
        out = None
        for s in range(3):
            term = tap[c, s, block : block + 1, :] * proj[c, pl.ds(8 + start - s, count), :]
            out = term if out is None else out + term
        return out

    def product(block, start, count):
        value = feature(block, 1, start, count) * feature(block, 2, start, count)
        kv[pl.ds(SPAN + start, count), :] = value.astype(jnp.bfloat16)

    def product_head(block, tile):
        product(block, tile * rows, 16)

    def product_rest(block, tile):
        product(block, tile * rows + 16, rows - 16)

    inside = (z > 0).astype(jnp.float32)

    def halo(block):
        a = remote(proj.at[:, pl.ds(total, 8)], rim.at[block], hsem.at[block, 0], hsem.at[block, 1], at["zp"])
        b = remote(kv.at[pl.ds(total, SPAN)], tail.at[block], hsem.at[block, 2], hsem.at[block, 3], at["zp"])
        return a, b

    group = lax.broadcasted_iota(jnp.int32, (SPAN, LANES), 1) // 16

    def conv(block, tile, target):
        start = tile * rows
        query = feature(block, 0, start, rows)
        wide = jnp.concatenate([kv[pl.ds(start + SPAN * b, 2 * SPAN), :] for b in range(3)], axis=1)
        out = jnp.dot(toep[block], wide, preferred_element_type=jnp.float32)
        for b in range(3):
            inner = jnp.zeros((SPAN, LANES), jnp.float32)
            for g in range(8):
                inner = jnp.where(group == g, out[SPAN * g : SPAN * (g + 1), LANES * b : LANES * (b + 1)], inner)
            value = (query[SPAN * b : SPAN * (b + 1)] * inner).astype(jnp.bfloat16)
            target[pl.ds(start + SPAN * b, SPAN), :] = value

    def take_rim(block, copy):
        copy.wait_recv()
        proj[:, pl.ds(0, 8), :] = rim[block] * inside

    def take_tail(block, copy):
        copy.wait_recv()
        kv[pl.ds(0, SPAN), :] = (tail[block].astype(jnp.float32) * inside).astype(jnp.bfloat16)

    def give(src, out, index, tile):
        d = (tile - y + NY) % NY
        part = src.at[pl.ds(tile * rows, rows)]
        dst = out.at[:, pl.ds(pl.multiple_of(y * LANES, LANES), LANES)]

        @pl.when(d == 0)
        def _():
            pltpu.make_async_copy(part, dst, lsem.at[3 + index]).start()

        @pl.when(d != 0)
        def _():
            remote(part, dst, osem.at[index, 0, d], osem.at[index, 1, d], {"seq": z * NY + tile}).start()

    def given(src, out, index):
        part = src.at[pl.ds(pl.multiple_of(y * rows, rows), rows)]
        cols = [out.at[:, pl.ds(pl.multiple_of(((y + NY - d) % NY) * LANES, LANES), LANES)] for d in range(NY)]
        pltpu.make_async_copy(part, cols[0], lsem.at[3 + index]).wait()
        for d in (1, 3, 2):
            copy = remote(part, cols[d], osem.at[index, 0, d], osem.at[index, 1, d], at["y%d" % d])
            copy.wait_recv()
            copy.wait_send()

    half_rows = rows // 2
    lo, hi = pl.ds(0, half_rows), pl.ds(half_rows, half_rows)
    after, before = (y + 1) % NY, (y + NY - 1) % NY

    def pass_on(tile, k):
        src, dst, where = (
            (part.at[tile, (y + 2) % NY, lo], relayed.at[tile, 0], "yp"),
            (part.at[tile, (y + 2) % NY, hi], relayed.at[tile, 1], "ym"),
            (part.at[tile, after, hi], summed.at[tile, 0, hi], "yp"),
            (part.at[tile, before, lo], summed.at[tile, 1, lo], "ym"),
            (part.at[tile, after, lo], summed.at[tile, 0, lo], "yp"),
            (part.at[tile, before, hi], summed.at[tile, 1, hi], "ym"),
        )[k]
        return remote(src, dst, dsem.at[tile, 0, 0], dsem.at[tile, 1, min(k, 2)], at[where])

    def partial(tile):
        left = jnp.concatenate([ybuf[k, pl.ds(tile * rows, rows), :] for k in range(8)], axis=1)
        right = wo[:, 0].reshape(8 * LANES, 4 * LANES)
        acc = jnp.dot(left, right, preferred_element_type=jnp.float32)
        for q in range(NY):
            part[tile, q] = acc[:, LANES * q : LANES * (q + 1)].astype(jnp.bfloat16)
        for k in range(4):
            pass_on(tile, k).start()

    def relay(tile):
        f32 = jnp.float32
        for k, to, span in ((0, after, lo), (1, before, hi)):
            pass_on(tile, k).wait_recv()
            value = part[tile, to, span, :].astype(f32) + relayed[tile, k].astype(f32)
            part[tile, to, span, :] = value.astype(jnp.bfloat16)
            pass_on(tile, 4 + k).start()

    def passed(tile):
        ref = part.at[tile, pl.ds(0, 3)]
        remote(ref, ref, dsem.at[tile, 0, 0], dsem.at[tile, 1, 0], at["yp"]).wait_send()

    def final(tile):
        f32 = jnp.float32
        ref = summed.at[tile]
        remote(ref, ref, dsem.at[tile, 0, 0], dsem.at[tile, 1, 2], at["yp"]).wait_recv()
        old = xbuf[mp * NY + tile, pl.ds(pl.multiple_of(y * rows, rows), rows), :]
        value = old.astype(f32) + part[tile, y].astype(f32)
        value = value + (summed[tile, 0].astype(f32) + summed[tile, 1].astype(f32))
        sbuf[own, pl.ds(tile * rows, rows), :] = value.astype(jnp.bfloat16)

    def pair(streams):
        p, q = (stream.steps() for stream in streams)

        def both(i):
            def run():
                p[i]()
                q[i]()
            return run

        return p, q, [both(i) for i in range(len(p))]

    for c in loads[4:]:
        c.wait()
    scale(0)
    for c in loads[:4]:
        c.wait()
    pl.semaphore_wait(barrier, len(peers))

    rings[0].trade()
    _, _, tk = pair(token_streams)
    tk[0]()
    rings[1].keep()
    scale(1)
    spread()
    build(0)
    for run in (rs[0][0], tk[1], tk[2], rs[0][1], tk[3], tk[4], tk[5], tk[6], rs[0][2], tk[7], tk[8], tk[9], rs[0][3]):
        run()
    rs[1][0]()
    tk[10]()
    tk[11]()
    rings[2].trade()
    build(1)
    lax.fori_loop(0, 4, project_near, 0)
    rs[0][4]()

    first_out = ybuf.at[mp]
    rim_copy, tail_copy = halo(0)
    ys = [stream.steps() for stream in mix_streams]
    s0, s1, sa = pair(next_streams[:2])
    s2, s3, sb = pair(next_streams[2:])
    project_far(3)
    rim_copy.start()
    product_rest(0, 3)
    tail_copy.start()
    rs[1][1]()
    project_far(0)
    rs[2][0]()
    take_rim(0, rim_copy)
    product(0, 0, rows)
    take_tail(0, tail_copy)
    conv(0, 0, first_out)
    ys[0][0]()
    rs[1][2]()
    project_far(1)
    product(0, rows, rows)
    conv(0, 1, first_out)
    ys[1][0]()
    ys[0][1]()
    rs[1][3]()
    project_far(2)
    product(0, 2 * rows, rows + 16)
    conv(0, 2, first_out)
    ys[2][0]()
    ys[0][2]()
    ys[1][1]()
    conv(0, 3, first_out)
    ys[3][0]()
    ys[0][3]()
    rim_copy.wait_send()
    tail_copy.wait_send()
    rs[1][4]()
    partial(0)
    ys[1][2]()
    ys[2][1]()
    rs[2][1]()
    ys[1][3]()
    partial(1)
    relay(0)
    ys[2][2]()
    ys[3][1]()
    ys[2][3]()
    partial(2)
    relay(1)
    ys[3][2]()
    final(0)
    s0[0]()
    ys[3][3]()
    partial(3)
    relay(2)
    final(1)
    s1[0]()
    relay(3)
    sa[1]()
    final(2)
    s2[0]()
    rs[2][2]()
    final(3)
    s3[0]()

    sa[2]()
    sb[1]()
    sa[3]()
    sa[4]()
    sb[2]()
    sa[5]()
    rs[2][3]()
    sb[3]()
    sa[6]()
    sb[4]()
    sa[7]()
    sb[5]()
    sa[8]()
    for stream in token_streams + mix_streams:
        stream.drain()
    for r in rings[:2]:
        r.drain()
    for tile in range(4):
        passed(tile)
    sb[6]()
    sa[9]()
    rs[2][4]()
    sa[10]()
    sb[7]()
    sa[11]()
    project(0)
    sb[8]()
    sb[9]()
    project(1)
    sb[10]()
    product_rest(1, 0)
    product(1, rows, rows)
    conv(1, 1, mix)
    give(mix, mixed_ref, 1, 1)
    sb[11]()
    for tile in range(4):
        give(sbuf.at[own], stream_ref, 0, tile)
    rim_copy, tail_copy = halo(1)
    project(3)
    rim_copy.start()
    product_rest(1, 3)
    tail_copy.start()
    project(2)
    product(1, 2 * rows, rows + 16)
    conv(1, 3, mix)
    give(mix, mixed_ref, 1, 3)
    conv(1, 2, mix)
    give(mix, mixed_ref, 1, 2)
    take_rim(1, rim_copy)
    product_head(1, 0)
    take_tail(1, tail_copy)
    conv(1, 0, mix)
    give(mix, mixed_ref, 1, 0)
    given(sbuf.at[own], stream_ref, 0)
    rim_copy.wait_send()
    tail_copy.wait_send()
    for stream in next_streams:
        stream.drain()
    rings[2].drain()
    given(mix, mixed_ref, 1)


def local(tokens, norm_gain, in_weight, feat_filter, short_filter, medium_filter, out_weight):
    rows, cols = tokens.shape
    taps = jnp.transpose(feat_filter, (1, 2, 0, 3))
    short = short_filter.T
    total = rows * NY
    bf16, f32 = jnp.bfloat16, jnp.float32
    out = jax.ShapeDtypeStruct((rows, cols), bf16)
    any_spec = pl.BlockSpec(memory_space=pl.ANY)
    return pl.pallas_call(
        kernel,
        out_shape=(out, out),
        in_specs=[any_spec] * 7,
        out_specs=(any_spec, any_spec),
        scratch_shapes=[
            pltpu.VMEM((32, total, LANES), bf16),
            pltpu.VMEM((8, total, LANES), bf16),
            pltpu.VMEM((32, total, LANES), bf16),
            pltpu.VMEM((NZ, 3, 512, LANES), bf16),
            pltpu.VMEM((NZ, 1, LANES, cols), bf16),
            pltpu.VMEM((NZ, 3, 512, LANES), bf16),
            pltpu.VMEM((7, 128, cols), bf16),
            pltpu.VMEM((2, LANES), f32),
            pltpu.VMEM((3, 3, 2, LANES), f32),
            pltpu.VMEM(short.shape, f32),
            pltpu.VMEM((LANES, LANES), f32),
            pltpu.VMEM((2, 8, SPAN), f32),
            pltpu.VMEM((2, 8 * SPAN, 2 * SPAN), bf16),
            pltpu.VMEM((3, 8 + total, LANES), f32),
            pltpu.VMEM((2, 3, 8, LANES), f32),
            pltpu.VMEM((2, SPAN, LANES), bf16),
            pltpu.VMEM((SPAN + total, LANES), bf16),
            pltpu.VMEM((total, LANES), bf16),
            pltpu.VMEM((total, LANES), f32),
            pltpu.VMEM((NY, NY, rows, LANES), bf16),
            pltpu.VMEM((NY, 2, rows // 2, LANES), bf16),
            pltpu.VMEM((NY, 2, rows, LANES), bf16),
            pltpu.SemaphoreType.DMA((10, 2, 16)),
            pltpu.SemaphoreType.DMA((3, 2, 28)),
            pltpu.SemaphoreType.DMA((2, 4)),
            pltpu.SemaphoreType.DMA((2, 2, 4)),
            pltpu.SemaphoreType.DMA((NY, 2, 3)),
            pltpu.SemaphoreType.DMA((11,)),
        ],
        compiler_params=pltpu.CompilerParams(
            collective_id=0, has_side_effects=True, vmem_limit_bytes=62 << 20
        ),
        name="hyena",
    )(tokens, norm_gain, in_weight, taps, short, medium_filter, out_weight)


def solution(mesh):
    placed = (
        P("seq", "mp"),
        P(),
        P(None, None, "seq", "mp"),
        P(None, None, None, "mp"),
        P("mp", None),
        P("mp", None),
        P("seq", "mp"),
    )
    return jax.shard_map(
        local,
        mesh=mesh,
        in_specs=placed,
        out_specs=(P("seq", "mp"), P("seq", "mp")),
        check_vma=False,
    )
```

time: 168 us -> 152 us (0.905)
  Pallas kernels: 161 us -> 149 us
  local copies, waits for them, and re-layouts: 4.83 us -> 2.57 us
    pallas_call x1, Pallas kernels: 161 us -> 149 us  [local(): pl.pallas_call(kernel, out_shape=(out, out), in_specs=[any_spec] * 7, out...]
    unnamed x8 -> x4, local copies, waits for them, and re-layouts: 4.19 us -> 2.57 us
where the time goes in v3:
time: 152 us
  Pallas kernels  149 us (98%)
  local copies, waits for them, and re-layouts  2.57 us (2%)
    pallas_call x1, Pallas kernels, local(): pl.pallas_call(kernel, out_shape=(out, out), in_specs=[any_spec] * 7, out...  149 us

profile of v3, /device:TPU:1, one launch (start us, length us, event | category | flops | bytes accessed | tf_op | source)
XLA Modules:
  0.0 151.9 jit_solution(10768648645674351835)
XLA Ops:
  0.6 148.7 %hyena.1 = (bf16[384,512]{1,0:T(8,128)(2,1)}, bf16[384,512]{1,0:T(8,128)(2,1)}) custom-call(bf16[384,512]{1,0:T(8,128)(2,1)} %tok.1, f32[2,4096]{1,0:T(2,128)} %gain.1, bf16[2,3,128,512]{3,2,1,0:T(8,128)(2,1)} %w_in.1, f32[3,3,2,512]{3,2,1,0:T(2,128)} %bitcast.2, f32[7,32]{1,0:T(8,128)} %bitcast.3, f32[32,128]{1,0:T(8,128)} %medium.1, bf16[128,512]{1,0:T(8,128)(2,1)} %w_out.1), custom_call_target="tpu_custom_call" | custom-call | tf_op jit(solution)/shard_map/hyena/pallas_call | solution.py:622
  149.3 0.0 copy-start
  149.3 1.8 %copy.11 = bf16[384,512]{1,0:T(8,128)(2,1)} copy(bf16[384,512]{1,0:T(8,128)(2,1)} %get-tuple-element.4) | data formatting | bytes 786432
  151.1 0.0 copy-done
  151.1 0.7 copy.12
Async XLA Ops:
  149.3 1.8 %copy-start = (bf16[384,512]{1,0:T(8,128)(2,1)S(1)}, bf16[384,512]{1,0:T(8,128)(2,1)}, u32[]{:S(2)}) copy-start(bf16[384,512]{1,0:T(8,128)(2,1)} %get-tuple-element.5) | copy-start | bytes 1179652

commit v4 on v3

--- a/solution.py
+++ b/solution.py
@@ -70,16 +70,6 @@
     def hand(self, off):
         self.handing(self.buf.at[self.slot(*self.place(off), self.at["core"]), self.span("all")]).start()
 
-    def hand_column(self, a):
-        if self.part == 0:
-            at = self.at
-            column = ((at["x"] + a + NX) % NX) * 2 + at["core"]
-            self.handing(self.buf.at[pl.ds(column * NY, NY), self.span("all")]).start()
-
-    def hand_now(self, off):
-        if self.part == 1 or self.flat:
-            self.hand(off)
-
     def steps(self):
         first_axis, second_axis = ((0, 1), (0, -1)), () if self.flat else ((1, 1), (1, -1))
 
@@ -89,7 +79,7 @@
         def begin():
             for step in first_axis + second_axis:
                 self.send(step, (0, 0), "all")
-            self.hand_now((0, 0))
+            self.hand((0, 0))
 
         def first():
             for sign in (1, -1):
@@ -97,27 +87,26 @@
                 self.send((0, sign), (-sign, 0), piece(sign))
                 for step in second_axis:
                     self.send(step, (-sign, 0), "all")
-                self.hand_now((-sign, 0))
+                self.hand((-sign, 0))
 
         def across(a):
             def run():
                 for sign in (1, -1):
                     self.receive((1, sign), (a, 0), "all")
                     self.send((1, sign), (a, -sign), piece(sign))
-                    self.hand_now((a, -sign))
+                    self.hand((a, -sign))
             return run
 
         def far():
             self.receive((0, 1), (-1, 0), "lo")
             for step in second_axis:
                 self.send(step, (2, 0), "all")
-            self.hand_now((2, 0))
+            self.hand((2, 0))
 
         def last(a):
             def run():
                 self.receive((1, 1), (a, -1), "lo")
-                self.hand_now((a, 2))
-                self.hand_column(a)
+                self.hand((a, 2))
             return run
 
         def end():
@@ -497,13 +486,13 @@
     rs[1][1]()
     project_far(0)
     rs[2][0]()
+    project_far(1)
     take_rim(0, rim_copy)
     product(0, 0, rows)
     take_tail(0, tail_copy)
     conv(0, 0, first_out)
     ys[0][0]()
     rs[1][2]()
-    project_far(1)
     product(0, rows, rows)
     conv(0, 1, first_out)
     ys[1][0]()

time: 152 us -> 151 us (level)
  no operation moved by 1% of the time
where the time goes in v4:
time: 151 us
  Pallas kernels  148 us (98%)
  local copies, waits for them, and re-layouts  2.57 us (2%)
    pallas_call x1, Pallas kernels, local(): pl.pallas_call(kernel, out_shape=(out, out), in_specs=[any_spec] * 7, out...  148 us

profile of v4, /device:TPU:1, one launch (start us, length us, event | category | flops | bytes accessed | tf_op | source)
XLA Modules:
  0.0 151.1 jit_solution(3114413481399026656)
XLA Ops:
  0.6 147.8 %hyena.1 = (bf16[384,512]{1,0:T(8,128)(2,1)}, bf16[384,512]{1,0:T(8,128)(2,1)}) custom-call(bf16[384,512]{1,0:T(8,128)(2,1)} %tok.1, f32[2,4096]{1,0:T(2,128)} %gain.1, bf16[2,3,128,512]{3,2,1,0:T(8,128)(2,1)} %w_in.1, f32[3,3,2,512]{3,2,1,0:T(2,128)} %bitcast.2, f32[7,32]{1,0:T(8,128)} %bitcast.3, f32[32,128]{1,0:T(8,128)} %medium.1, bf16[128,512]{1,0:T(8,128)(2,1)} %w_out.1), custom_call_target="tpu_custom_call" | custom-call | tf_op jit(solution)/shard_map/hyena/pallas_call | solution.py:611
  148.5 0.0 copy-start
  148.5 1.8 %copy.11 = bf16[384,512]{1,0:T(8,128)(2,1)} copy(bf16[384,512]{1,0:T(8,128)(2,1)} %get-tuple-element.4) | data formatting | bytes 786432
  150.3 0.0 copy-done
  150.3 0.7 copy.12
Async XLA Ops:
  148.5 1.8 %copy-start = (bf16[384,512]{1,0:T(8,128)(2,1)S(1)}, bf16[384,512]{1,0:T(8,128)(2,1)}, u32[]{:S(2)}) copy-start(bf16[384,512]{1,0:T(8,128)(2,1)} %get-tuple-element.5) | copy-start | bytes 1179652
